TPU v7x, 32 devices: a whole 2x2x4 slice. The times are simulated.
32 devices in a mesh: lon: 16 (over z, x, core), lat: 2 (over y).
Axes of the slice: x: 2, y: 2, z: 4, core: 2. Of those that a mesh axis runs over, the one named last changes fastest.
Arguments:
- state: float32 [5, 1, 5760, 256], P(None, None, 'lon', 'lat'), may hold values from -3 to 3
- cutoffs: int32 [2, 128], replicated, may hold values from 1 to 2879, as said below
Outputs:
- advanced: float32 [5, 1, 5760, 256], P(None, None, 'lon', 'lat')
Inputs may be any that keep to these rules, and one draw needn't show every extreme that they name: cutoffs[0, j] is the highest zonal wavenumber kept in row j and cutoffs[1, j] that of row 255 - j; in both caps the row at the pole keeps 1 and row 127 from the pole keeps 2880 - 1.
All inputs are finite; a program needn't handle non-finite values.
Results may differ from a plain program's by a relative error of at most 0.0003.
Values sent between devices are 32-bit elements; how exact they have to be, the bound alone decides.
A program may use at most 64 MiB of HBM per device.

v0:
```python
import jax
import jax.numpy as jnp
from jax import lax
from jax.sharding import PartitionSpec as P

SUBSTEPS = 2
time_step = 0.5
gravity_scale = 0.25
coriolis_scale = 0.5
wind_sign = (1.0, -1.0, -1.0, 1.0, 1.0)
highest = lax.Precision.HIGHEST
inner_factor = 64


def passed_along(value, axis, steps):
    count = lax.axis_size(axis)
    pairs = [(source, (source + steps) % count) for source in range(count)]
    return lax.ppermute(value, axis, pairs)


def extended(array, sides, width, wrap):
    for axis, dim in sides:
        peers, length = (lax.axis_size(axis), array.shape[dim])
        up = [(i, (i + 1) % peers) for i in range(peers if wrap else peers - 1)]
        down = [(j, i) for i, j in up]
        last = lax.slice_in_dim(array, length - width, length, axis=dim)
        initial = lax.slice_in_dim(array, 0, width, axis=dim)
        before = lax.ppermute(last, axis, up)
        after = lax.ppermute(initial, axis, down)
        array = jnp.concatenate([before, array, after], axis=dim)
    return array


def interface_flux(halo_padded, transported_field, advection_axis, extent_length):

    def shifted(offset):
        return lax.slice_in_dim(
            halo_padded, offset, offset + extent_length + 1, axis=advection_axis
        )

    far_west, mid_west, near_west, centre, near_east, far_east = [
        shifted(offset) for offset in range(6)
    ]
    interface_velocity = 0.5 * (
        lax.slice_in_dim(transported_field, 2, extent_length + 3, axis=advection_axis)
        + lax.slice_in_dim(transported_field, 3, extent_length + 4, axis=advection_axis)
    )
    central = (
        37.0 * (centre + near_west) - 8.0 * (near_east + mid_west) + (far_east + far_west)
    ) / 60.0
    upwind = (
        far_east - far_west - 5.0 * (near_east - mid_west) + 10.0 * (centre - near_west)
    ) / 60.0
    return interface_velocity * central - jnp.abs(interface_velocity) * upwind


def latitude_rows(first_row, row_count, total_rows):
    centres = (first_row + jnp.arange(row_count, dtype=jnp.int32)).astype(jnp.float32) + 0.5
    centre_cos = jnp.sin(centres * (jnp.pi / total_rows))
    centre_sin = -jnp.cos(centres * (jnp.pi / total_rows))
    faces = first_row + jnp.arange(row_count + 1, dtype=jnp.int32)
    face_cos = jnp.sin(
        jnp.minimum(faces, total_rows - faces).astype(jnp.float32) * (jnp.pi / total_rows)
    )
    return (centre_cos, centre_sin, face_cos)


def geopotential(fields):
    layer_mass = fields[0] * fields[3]
    return gravity_scale * jnp.flip(jnp.cumsum(jnp.flip(layer_mass, 0), axis=0), 0)


def zonal_tendency(lon_padded, centre_cos):
    lon_cells = lon_padded.shape[2] - 6
    face_fluxes = interface_flux(lon_padded, lon_padded[1:2], 2, lon_cells)
    zonal = face_fluxes[:, :, :-1] - face_fluxes[:, :, 1:]
    height = geopotential(lon_padded)
    height_slope = 0.5 * (height[:, 4 : lon_cells + 4] - height[:, 2 : lon_cells + 2])
    zonal = jnp.concatenate([zonal[:1], zonal[1:2] - height_slope[None], zonal[2:]], axis=0)
    return zonal / centre_cos


def phase_table(first, second, modulus, total):
    angle = (first[:, None] * second[None, :] % modulus).astype(jnp.float32) * (
        2.0 * jnp.pi / total
    )
    return (jnp.cos(angle), jnp.sin(angle))


def truncate_rows(rows, row_limit, lon_total):
    row_count = rows.shape[0]
    outer = lon_total // inner_factor
    outer_index = jnp.arange(outer, dtype=jnp.int32)
    inner_index = jnp.arange(inner_factor, dtype=jnp.int32)
    outer_cos, outer_sin = phase_table(outer_index, outer_index, outer, outer)
    twist_cos, twist_sin = phase_table(outer_index, inner_index, lon_total, lon_total)
    inner_cos, inner_sin = phase_table(inner_index, inner_index, inner_factor, inner_factor)
    folded = rows.reshape(row_count, outer, inner_factor)
    first_re = jnp.einsum("rpq,pk->rkq", folded, outer_cos, precision=highest)
    first_im = -jnp.einsum("rpq,pk->rkq", folded, outer_sin, precision=highest)
    turned_re = first_re * twist_cos + first_im * twist_sin
    turned_im = first_im * twist_cos - first_re * twist_sin
    spec_re = jnp.einsum("rkq,qj->rkj", turned_re, inner_cos, precision=highest) + jnp.einsum(
        "rkq,qj->rkj", turned_im, inner_sin, precision=highest
    )
    spec_im = jnp.einsum("rkq,qj->rkj", turned_im, inner_cos, precision=highest) - jnp.einsum(
        "rkq,qj->rkj", turned_re, inner_sin, precision=highest
    )
    wave = outer_index[:, None] + outer * inner_index[None, :]
    wave = jnp.minimum(wave, lon_total - wave).astype(jnp.float32)
    kept = wave[None, :, :] <= row_limit[:, None, None]
    spec_re = jnp.where(kept, spec_re, 0.0)
    spec_im = jnp.where(kept, spec_im, 0.0)
    back_re = jnp.einsum("rkj,qj->rkq", spec_re, inner_cos, precision=highest) - jnp.einsum(
        "rkj,qj->rkq", spec_im, inner_sin, precision=highest
    )
    back_im = jnp.einsum("rkj,qj->rkq", spec_re, inner_sin, precision=highest) + jnp.einsum(
        "rkj,qj->rkq", spec_im, inner_cos, precision=highest
    )
    untwist_re = back_re * twist_cos - back_im * twist_sin
    untwist_im = back_re * twist_sin + back_im * twist_cos
    result = jnp.einsum("rkq,pk->rpq", untwist_re, outer_cos, precision=highest) - jnp.einsum(
        "rkq,pk->rpq", untwist_im, outer_sin, precision=highest
    )
    return result.reshape(row_count, lon_total) / lon_total


def crossing_rims(state, is_south, is_north):
    lat_cells = state.shape[3]
    lon_count = lax.axis_size("lon")
    wind_flip = jnp.array(wind_sign, dtype=jnp.float32)[:, None, None, None]
    pole_rows = jnp.where(is_south, state[..., 0:2], state[..., lat_cells - 2 :])
    partner = passed_along(pole_rows, "lon", lon_count // 2) * wind_flip
    lat_halo = extended(state, (("lat", 3),), 3, False)
    south_rim = jnp.where(
        is_south,
        jnp.concatenate([lat_halo[..., 0:1], partner[..., 1:2], partner[..., 0:1]], axis=3),
        lat_halo[..., 0:3],
    )
    north_rim = jnp.where(
        is_north,
        jnp.concatenate(
            [partner[..., 1:2], partner[..., 0:1], lat_halo[..., lat_cells + 5 :]], axis=3
        ),
        lat_halo[..., lat_cells + 3 :],
    )
    return jnp.concatenate([south_rim, state, north_rim], axis=3)


def advance(state, geometry, cutoff_row, is_south, is_north):
    centre_cos, centre_sin, face_cos = geometry
    field_count, level_count, lon_cells, lat_cells = state.shape
    lon_count = lax.axis_size("lon")
    lon_total = lon_cells * lon_count
    lon_padded = extended(state, (("lon", 2),), 3, True)
    zonal = zonal_tendency(lon_padded, centre_cos)
    row_block = jnp.transpose(zonal, (0, 1, 3, 2)).reshape(lon_count, -1, lon_cells)
    row_limits = jnp.broadcast_to(cutoff_row, (field_count, level_count, lat_cells)).reshape(
        lon_count, -1, 1
    )
    values = lax.all_to_all(row_block, "lon", split_axis=0, concat_axis=2, tiled=True)
    limits = lax.all_to_all(row_limits, "lon", split_axis=0, concat_axis=2, tiled=True)
    spread = truncate_rows(values[0], limits[0, :, 0], lon_total)[None]
    returned = lax.all_to_all(spread, "lon", split_axis=2, concat_axis=0, tiled=True)
    filtered = jnp.transpose(
        returned.reshape(field_count, level_count, lat_cells, lon_cells), (0, 1, 3, 2)
    )
    zonal = jnp.where(jnp.logical_or(is_south, is_north), filtered, zonal)
    lat_padded = crossing_rims(state, is_south, is_north)
    merid_fluxes = interface_flux(lat_padded, lat_padded[2:3], 3, lat_cells) * face_cos
    meridional = (merid_fluxes[..., :-1] - merid_fluxes[..., 1:]) / centre_cos
    height = geopotential(lat_padded)
    north_slope = 0.5 * (height[..., 4 : lat_cells + 4] - height[..., 2 : lat_cells + 2])
    turning = coriolis_scale * centre_sin
    flux_tendency = zonal + meridional
    east_wind = flux_tendency[1] + turning * state[2]
    north_wind = flux_tendency[2] - turning * state[1] - north_slope
    flux_tendency = jnp.concatenate(
        [flux_tendency[:1], east_wind[None], north_wind[None], flux_tendency[3:]], axis=0
    )
    return state + time_step * flux_tendency


def shards(state, cutoffs):
    lat_index = lax.axis_index("lat")
    lat_count = lax.axis_size("lat")
    lat_cells = state.shape[3]
    geometry = latitude_rows(lat_index * lat_cells, lat_cells, lat_cells * lat_count)
    is_south = lat_index == 0
    is_north = lat_index == lat_count - 1
    north_row = jnp.where(is_north, jnp.flip(cutoffs[1], 0), -1)
    cutoff_row = jnp.where(is_south, cutoffs[0], north_row).astype(jnp.float32)
    for substep_index in range(SUBSTEPS):
        state = advance(state, geometry, cutoff_row, is_south, is_north)
    return state


def solution(mesh):
    return jax.shard_map(
        shards,
        mesh=mesh,
        in_specs=(P(None, None, "lon", "lat"), P()),
        out_specs=P(None, None, "lon", "lat"),
        check_vma=False,
    )
```

profile of v0, /device:TPU:9, one launch (start us, length us, event | category | flops | bytes accessed | tf_op | source)
XLA Modules:
  0.0 308.5 jit_solution(16900312575509501687)
XLA Ops:
  4.8 8.6 %all-to-all-start = ((f32[16,40,1]{1,2,0:T(1,128)}), f32[16,40,1]{1,2,0:T(1,128)S(1)}, u32[]{:S(2)}, u32[]{:S(2)}) async-start(f32[16,40,1]{1,2,0:T(1,128)} %bitcast.2), calls=%async_computation | async-start | bytes 16384 | tf_op jit(solution)/shard_map/all_to_all | solution.py:162
  18.1 5.3 %all-to-all-start.1 = ((f32[16,40,360]{2,1,0:T(8,128)}), f32[16,40,360]{2,1,0:T(8,128)S(1)}, u32[]{:S(2)}, u32[]{:S(2)}) async-start(f32[16,40,360]{2,1,0:T(8,128)} %bitcast.260), calls=%async_computation.1 | async-start | bytes 1966080 | tf_op jit(solution)/shard_map/all_to_all | solution.py:161
  24.6 1.5 copy.215
  26.1 2.1 collective-permute-start.2
  28.2 1.5 fusion.274
  29.7 1.5 copy.269
  32.5 1.5 copy.270
  34.0 4.0 %collective-permute-start.4 = (f32[5,1,360,3]{2,1,3,0:T(1,128)S(1)}, f32[5,1,360,3]{2,1,3,0:T(1,128)S(1)}, u32[]{:S(2)}, u32[]{:S(2)}) collective-permute-start(f32[5,1,360,3]{2,1,3,0:T(1,128)S(1)} %copy.270), channel_id=1, source_target_pairs={{0,1},{2,3},{4,5},{6,7},{8,9},{10,11},{12,13},{14,15},{16,17},{18,... | collective-permute-start | bytes 64808 | tf_op jit(solution)/shard_map/ppermute | solution.py:28
  38.4 8.9 %all-to-all-done.1 = f32[16,40,360]{2,1,0:T(8,128)S(1)} async-done(((f32[16,40,360]{2,1,0:T(8,128)}), f32[16,40,360]{2,1,0:T(8,128)S(1)}, u32[]{:S(2)}, u32[]{:S(2)}) %all-to-all-start.1) | async-done | bytes 921632 | tf_op jit(solution)/shard_map/all_to_all | solution.py:161
  48.4 3.4 %reshape_squeeze.6 = f32[40,90,64]{2,1,0:T(8,128)} reshape(f32[1,40,16,360]{3,2,1,0:T(8,128)} %copy.204) | data formatting | bytes 1843200 | tf_op jit(solution)/shard_map/reshape;squeeze | solution.py:98
  51.8 2.1 copy.205
  53.9 1.4 fusion.84
  56.7 1.6 fusion.18
  58.4 1.6 fusion.22
  60.0 1.8 compare_select_fusion.3
  63.2 1.4 fusion.106
  64.6 1.8 compare_select_fusion.2
  66.4 1.8 convolution_subtract_fusion.2
  68.2 1.8 multiply_add_fusion.2
  70.0 1.4 fusion.82
  71.5 1.4 fusion.90
  73.1 3.6 %copy.259 = f32[40,90,64]{0,2,1:T(8,128)} copy(f32[40,90,64]{1,2,0:T(8,128)S(1)} %multiply_bitcast_fusion.1) | data formatting | bytes 1843200 | tf_op jit(solution)/shard_map/div | solution.py:125
  77.3 27.7 %reduce = f32[5760,40]{1,0:T(8,128)} reduce(f32[5760,1,40]{2,1,0:T(1,128)} %bitcast.246, f32[]{:T(128)} %broadcast.641), dimensions={1}, to_apply=%bitcast.202.reduce_sub_computation | reduce | bytes 1843204
  105.0 4.8 %reshape.638 = f32[16,1,14400]{2,1,0:T(1,128)} reshape(f32[5760,40]{1,0:T(8,128)} %reduce) | data formatting | bytes 1843200
  109.8 5.3 %all-to-all-start.2 = ((f32[16,1,14400]{2,1,0:T(1,128)}), f32[16,1,14400]{2,1,0:T(1,128)}, u32[]{:S(2)}, u32[]{:S(2)}) async-start(f32[16,1,14400]{2,1,0:T(1,128)} %reshape.638), calls=%async_computation.2 | async-start | bytes 1851392 | tf_op jit(solution)/shard_map/all_to_all | solution.py:164
  121.0 2.8 maximum_select_fusion.1
  125.2 3.6 %subtract_multiply_fusion.1 = f32[5,1,360,129]{3,2,1,0:T(8,128)S(1)} fusion(f32[5,1,360,3]{3,2,1,0:T(8,128)S(1)} %get-tuple-element.20, f32[5,1,360,128]{3,2,1,0:T(8,128)S(1)} %copy-done, f32[5,1,360,3]{3,2,1,0:T(8,128)S(1)} %get-tuple-element.19, f32[129]{0:T(256)S(1)} %fusion.173, f32[360,129]{1,0:T(8,128)S(1)} %multiply_bitcast_fusion.4, ...), kind=kLoop, calls=%fused_computation.41 | loop fusion | flops 5572800 | bytes 2265636 | tf_op jit(solution)/shard_map/mul | solution.py:170
  128.8 8.7 %all-to-all-done.2 = f32[16,1,14400]{2,1,0:T(1,128)} async-done(((f32[16,1,14400]{2,1,0:T(1,128)}), f32[16,1,14400]{2,1,0:T(1,128)}, u32[]{:S(2)}, u32[]{:S(2)}) %all-to-all-start.2) | async-done | bytes 921632 | tf_op jit(solution)/shard_map/all_to_all | solution.py:164
  137.5 4.9 %reduce.1 = f32[16,14400]{1,0:T(8,128)} reduce(f32[16,1,14400]{2,1,0:T(1,128)} %all-to-all-done.2, f32[]{:T(128)} %broadcast.641), dimensions={1}, to_apply=%all_to_all.69.reduce_sub_computation | reduce | bytes 1843204 | tf_op jit(solution)/shard_map/all_to_all | solution.py:164
  142.4 8.8 %reshape.639 = f32[5760,1,40]{2,1,0:T(1,128)} reshape(f32[16,14400]{1,0:T(8,128)} %reduce.1) | data formatting | bytes 1843200
  151.2 3.1 copy.213
  154.3 2.5 copy.214
  156.7 1.7 fusion.36
  159.8 2.1 collective-permute-start.6
  165.4 9.8 %all-to-all-start.3 = ((f32[16,40,360]{2,1,0:T(8,128)}), f32[16,40,360]{2,1,0:T(8,128)S(1)}, u32[]{:S(2)}, u32[]{:S(2)}) async-start(f32[16,40,360]{2,1,0:T(8,128)} %bitcast.261), calls=%async_computation.3 | async-start | bytes 1966080 | tf_op jit(solution)/shard_map/all_to_all | solution.py:161
  175.2 1.5 fusion.270
  176.8 1.5 copy.241
  179.6 1.5 copy.244
  181.0 4.0 %collective-permute-start.9 = (f32[5,1,360,3]{2,1,3,0:T(1,128)S(1)}, f32[5,1,360,3]{2,1,3,0:T(1,128)S(1)}, u32[]{:S(2)}, u32[]{:S(2)}) collective-permute-start(f32[5,1,360,3]{2,1,3,0:T(1,128)S(1)} %copy.244), channel_id=1, source_target_pairs={{0,1},{2,3},{4,5},{6,7},{8,9},{10,11},{12,13},{14,15},{16,17},{18,... | collective-permute-start | bytes 64808 | tf_op jit(solution)/shard_map/ppermute | solution.py:28
  186.3 1.5 copy.237
  187.8 2.2 collective-permute-start.7
  190.0 9.3 %all-to-all-done.3 = f32[16,40,360]{2,1,0:T(8,128)S(1)} async-done(((f32[16,40,360]{2,1,0:T(8,128)}), f32[16,40,360]{2,1,0:T(8,128)S(1)}, u32[]{:S(2)}, u32[]{:S(2)}) %all-to-all-start.3) | async-done | bytes 921632 | tf_op jit(solution)/shard_map/all_to_all | solution.py:161
  200.3 3.4 %reshape_squeeze.7 = f32[40,90,64]{2,1,0:T(8,128)} reshape(f32[1,40,16,360]{3,2,1,0:T(8,128)} %copy.226) | data formatting | bytes 1843200 | tf_op jit(solution)/shard_map/reshape;squeeze | solution.py:98
  203.7 1.9 copy.227
  208.4 1.6 fusion.12
  210.1 1.6 fusion.16
  211.7 1.8 compare_select_fusion.1
  214.9 1.4 fusion.103
  216.3 1.8 compare_select_fusion
  218.1 1.6 convolution_subtract_fusion
  219.7 1.8 multiply_add_fusion
  221.5 1.4 fusion.78
  223.0 1.4 fusion.86
  224.6 3.6 %copy.264 = f32[40,90,64]{0,2,1:T(8,128)} copy(f32[40,90,64]{1,2,0:T(8,128)S(1)} %multiply_bitcast_fusion) | data formatting | bytes 1843200 | tf_op jit(solution)/shard_map/div | solution.py:125
  228.2 27.7 %reduce.2 = f32[5760,40]{1,0:T(8,128)} reduce(f32[5760,1,40]{2,1,0:T(1,128)} %bitcast.248, f32[]{:T(128)} %broadcast.641), dimensions={1}, to_apply=%bitcast.204.reduce_sub_computation | reduce | bytes 1843204
  255.9 4.8 %reshape.640 = f32[16,1,14400]{2,1,0:T(1,128)} reshape(f32[5760,40]{1,0:T(8,128)} %reduce.2) | data formatting | bytes 1843200
  260.7 5.1 %all-to-all-start.4 = ((f32[16,1,14400]{2,1,0:T(1,128)}), f32[16,1,14400]{2,1,0:T(1,128)S(1)}, u32[]{:S(2)}, u32[]{:S(2)}) async-start(f32[16,1,14400]{2,1,0:T(1,128)} %reshape.640), calls=%async_computation.4 | async-start | bytes 1851392 | tf_op jit(solution)/shard_map/all_to_all | solution.py:164
  273.6 3.9 %maximum_select_fusion.3 = (f32[5,1,360,3]{3,2,1,0:T(8,128)S(1)}, f32[5,1,360,3]{3,2,1,0:T(8,128)S(1)}) fusion(f32[5,1,360,3]{3,2,1,0:T(8,128)} %copy.246, f32[5,1,360,1]{3,2,1,0:T(8,128)} %copy.272, f32[5,1,360,1]{3,2,1,0:T(8,128)} %copy.271, f32[5,1,360,1]{3,2,1,0:T(8,128)} %copy.245, pred[]{:T(512)S(6)} %eq.15, f32[5,1,360,3]{3,2,1,0:T(8,128)} %copy.243, ...), kind=kLoop, calls=%fused_computation.108 | loop fusion | flops 32400 | bytes 115202 | tf_op jit(solution)/shard_map/jit(_where)/select_n | solution.py:135
  278.1 4.5 %subtract_multiply_fusion = f32[5,1,360,129]{3,2,1,0:T(8,128)} fusion(f32[5,1,360,3]{3,2,1,0:T(8,128)S(1)} %get-tuple-element.18, f32[5,1,360,128]{3,2,1,0:T(8,128)S(1)} %fusion.37, f32[5,1,360,3]{3,2,1,0:T(8,128)S(1)} %get-tuple-element.17, f32[360,129]{1,0:T(8,128)S(1)} %multiply_bitcast_fusion.2, f32[360,129]{1,0:T(8,128)S(1)} %get-tuple-element.7, ...), kind=kLoop, calls=%fused_computation.40 | loop fusion | flops 5572800 | bytes 2265636 | tf_op jit(solution)/shard_map/mul | solution.py:170
  282.7 5.5 %all-to-all-done.4 = f32[16,1,14400]{2,1,0:T(1,128)S(1)} async-done(((f32[16,1,14400]{2,1,0:T(1,128)}), f32[16,1,14400]{2,1,0:T(1,128)S(1)}, u32[]{:S(2)}, u32[]{:S(2)}) %all-to-all-start.4) | async-done | bytes 921632 | tf_op jit(solution)/shard_map/all_to_all | solution.py:164
  288.2 4.1 %reduce.3 = f32[16,14400]{1,0:T(8,128)} reduce(f32[16,1,14400]{2,1,0:T(1,128)S(1)} %all-to-all-done.4, f32[]{:T(128)} %broadcast.641), dimensions={1}, to_apply=%all_to_all.75.reduce_sub_computation | reduce | bytes 1843204 | tf_op jit(solution)/shard_map/all_to_all | solution.py:164
  292.2 8.8 %reshape.641 = f32[5760,1,40]{2,1,0:T(1,128)} reshape(f32[16,14400]{1,0:T(8,128)} %reduce.3) | data formatting | bytes 1843200
  301.0 2.3 copy.235
  304.5 2.4 fusion.34
  (106 shorter events, 48.2 us)
Async XLA Ops:
  0.0 14.7 %copy-start = (f32[5,1,360,128]{3,2,1,0:T(8,128)S(1)}, f32[5,1,360,128]{3,2,1,0:T(8,128)}, u32[]{:S(2)}) copy-start(f32[5,1,360,128]{3,2,1,0:T(8,128)} %param.4) | copy-start | bytes 2764804
  0.8 13.9 %collective-permute-start = (f32[5,1,3,128]{3,2,1,0:T(4,128)S(1)}, f32[5,1,3,128]{3,2,1,0:T(4,128)S(1)}, u32[]{:S(2)}, u32[]{:S(2)}) collective-permute-start(f32[5,1,3,128]{3,2,1,0:T(4,128)S(1)} %get-tuple-element.33), channel_id=1, source_target_pairs={{2,0},{4,2},{6,4},{8,6},{10,8},{12,10},{14,12},{16,14},{18,16},{20... | collective-permute-start | bytes 23048 | tf_op jit(solution)/shard_map/ppermute | solution.py:29
  1.5 13.2 %collective-permute-start.1 = (f32[5,1,3,128]{3,2,1,0:T(4,128)S(1)}, f32[5,1,3,128]{3,2,1,0:T(4,128)S(1)}, u32[]{:S(2)}, u32[]{:S(2)}) collective-permute-start(f32[5,1,3,128]{3,2,1,0:T(4,128)S(1)} %get-tuple-element.34), channel_id=1, source_target_pairs={{0,2},{2,4},{4,6},{6,8},{8,10},{10,12},{12,14},{14,16},{16,18},{18... | collective-permute-start | bytes 23048 | tf_op jit(solution)/shard_map/ppermute | solution.py:28
  4.8 13.3 %all-to-all-start = ((f32[16,40,1]{1,2,0:T(1,128)}), f32[16,40,1]{1,2,0:T(1,128)S(1)}, u32[]{:S(2)}, u32[]{:S(2)}) async-start(f32[16,40,1]{1,2,0:T(1,128)} %bitcast.2), calls=%async_computation | async-start | bytes 16384 | tf_op jit(solution)/shard_map/all_to_all | solution.py:162
  15.9 1.4 copy-start.1
  15.9 1.4 copy-start.2
  18.1 29.2 %all-to-all-start.1 = ((f32[16,40,360]{2,1,0:T(8,128)}), f32[16,40,360]{2,1,0:T(8,128)S(1)}, u32[]{:S(2)}, u32[]{:S(2)}) async-start(f32[16,40,360]{2,1,0:T(8,128)} %bitcast.260), calls=%async_computation.1 | async-start | bytes 1966080 | tf_op jit(solution)/shard_map/all_to_all | solution.py:161
  26.1 89.0 %collective-permute-start.2 = (f32[5,1,360,2]{2,3,1,0:T(2,128)S(1)}, f32[5,1,360,2]{2,3,1,0:T(2,128)S(1)}, u32[]{:S(2)}, u32[]{:S(2)}) collective-permute-start(f32[5,1,360,2]{2,3,1,0:T(2,128)S(1)} %copy.215), channel_id=1, source_target_pairs={{0,16},{2,18},{4,20},{6,22},{8,24},{10,26},{12,28},{14,30},{16,0},... | collective-permute-start | bytes 43208 | tf_op jit(solution)/shard_map/ppermute | solution.py:18
  31.2 84.6 %collective-permute-start.3 = (f32[5,1,360,3]{2,1,3,0:T(1,128)S(1)}, f32[5,1,360,3]{2,1,3,0:T(1,128)S(1)}, u32[]{:S(2)}, u32[]{:S(2)}) collective-permute-start(f32[5,1,360,3]{2,1,3,0:T(1,128)S(1)} %copy.269), channel_id=1, source_target_pairs={{1,0},{3,2},{5,4},{7,6},{9,8},{11,10},{13,12},{15,14},{17,16},{19,... | collective-permute-start | bytes 64808 | tf_op jit(solution)/shard_map/ppermute | solution.py:29
  34.0 83.1 %collective-permute-start.4 = (f32[5,1,360,3]{2,1,3,0:T(1,128)S(1)}, f32[5,1,360,3]{2,1,3,0:T(1,128)S(1)}, u32[]{:S(2)}, u32[]{:S(2)}) collective-permute-start(f32[5,1,360,3]{2,1,3,0:T(1,128)S(1)} %copy.270), channel_id=1, source_target_pairs={{0,1},{2,3},{4,5},{6,7},{8,9},{10,11},{12,13},{14,15},{16,17},{18,... | collective-permute-start | bytes 64808 | tf_op jit(solution)/shard_map/ppermute | solution.py:28
  109.8 5.3 %copy-start.4 = (f32[5]{0:T(128)S(1)}, f32[5]{0:T(128)}, u32[]{:S(2)}) copy-start(f32[5]{0:T(128)} %constant.123.clone) | copy-start | bytes 64
  109.8 27.7 %all-to-all-start.2 = ((f32[16,1,14400]{2,1,0:T(1,128)}), f32[16,1,14400]{2,1,0:T(1,128)}, u32[]{:S(2)}, u32[]{:S(2)}) async-start(f32[16,1,14400]{2,1,0:T(1,128)} %reshape.638), calls=%async_computation.2 | async-start | bytes 1851392 | tf_op jit(solution)/shard_map/all_to_all | solution.py:164
  158.4 1.0 copy-start.3
  159.7 3.2 %collective-permute-start.5 = (f32[5,1,3,128]{3,2,1,0:T(4,128)S(1)}, f32[5,1,3,128]{3,2,1,0:T(4,128)S(1)}, u32[]{:S(2)}, u32[]{:S(2)}) collective-permute-start(f32[5,1,3,128]{3,2,1,0:T(4,128)S(1)} %get-tuple-element.26), channel_id=1, source_target_pairs={{2,0},{4,2},{6,4},{8,6},{10,8},{12,10},{14,12},{16,14},{18,16},{20... | collective-permute-start | bytes 23048 | tf_op jit(solution)/shard_map/ppermute | solution.py:29
  159.8 3.1 %collective-permute-start.6 = (f32[5,1,3,128]{3,2,1,0:T(4,128)S(1)}, f32[5,1,3,128]{3,2,1,0:T(4,128)S(1)}, u32[]{:S(2)}, u32[]{:S(2)}) collective-permute-start(f32[5,1,3,128]{3,2,1,0:T(4,128)S(1)} %get-tuple-element.25), channel_id=1, source_target_pairs={{0,2},{2,4},{4,6},{6,8},{8,10},{10,12},{12,14},{14,16},{16,18},{18... | collective-permute-start | bytes 23048 | tf_op jit(solution)/shard_map/ppermute | solution.py:28
  165.4 33.8 %all-to-all-start.3 = ((f32[16,40,360]{2,1,0:T(8,128)}), f32[16,40,360]{2,1,0:T(8,128)S(1)}, u32[]{:S(2)}, u32[]{:S(2)}) async-start(f32[16,40,360]{2,1,0:T(8,128)} %bitcast.261), calls=%async_computation.3 | async-start | bytes 1966080 | tf_op jit(solution)/shard_map/all_to_all | solution.py:161
  178.2 90.2 %collective-permute-start.8 = (f32[5,1,360,3]{2,1,3,0:T(1,128)S(1)}, f32[5,1,360,3]{2,1,3,0:T(1,128)S(1)}, u32[]{:S(2)}, u32[]{:S(2)}) collective-permute-start(f32[5,1,360,3]{2,1,3,0:T(1,128)S(1)} %copy.241), channel_id=1, source_target_pairs={{1,0},{3,2},{5,4},{7,6},{9,8},{11,10},{13,12},{15,14},{17,16},{19,... | collective-permute-start | bytes 64808 | tf_op jit(solution)/shard_map/ppermute | solution.py:29
  181.0 88.7 %collective-permute-start.9 = (f32[5,1,360,3]{2,1,3,0:T(1,128)S(1)}, f32[5,1,360,3]{2,1,3,0:T(1,128)S(1)}, u32[]{:S(2)}, u32[]{:S(2)}) collective-permute-start(f32[5,1,360,3]{2,1,3,0:T(1,128)S(1)} %copy.244), channel_id=1, source_target_pairs={{0,1},{2,3},{4,5},{6,7},{8,9},{10,11},{12,13},{14,15},{16,17},{18,... | collective-permute-start | bytes 64808 | tf_op jit(solution)/shard_map/ppermute | solution.py:28
  187.8 78.0 %collective-permute-start.7 = (f32[5,1,360,2]{2,3,1,0:T(2,128)S(1)}, f32[5,1,360,2]{2,3,1,0:T(2,128)S(1)}, u32[]{:S(2)}, u32[]{:S(2)}) collective-permute-start(f32[5,1,360,2]{2,3,1,0:T(2,128)S(1)} %copy.237), channel_id=1, source_target_pairs={{0,16},{2,18},{4,20},{6,22},{8,24},{10,26},{12,28},{14,30},{16,0},... | collective-permute-start | bytes 43208 | tf_op jit(solution)/shard_map/ppermute | solution.py:18
  260.7 27.5 %all-to-all-start.4 = ((f32[16,1,14400]{2,1,0:T(1,128)}), f32[16,1,14400]{2,1,0:T(1,128)S(1)}, u32[]{:S(2)}, u32[]{:S(2)}) async-start(f32[16,1,14400]{2,1,0:T(1,128)} %reshape.640), calls=%async_computation.4 | async-start | bytes 1851392 | tf_op jit(solution)/shard_map/all_to_all | solution.py:164
where the time goes:
time: 314 us; the launch traced here: 308 us
  other arithmetic  93.3 us (30%)
  local copies, waits for them, and re-layouts  89.5 us (29%)
  starting transfers between devices  53 us (17%)
  matrix products  37.6 us (12%)
  waiting for transfers between devices  34.1 us (11%)
    unnamed x2, other arithmetic  55.4 us
    unnamed x22, local copies, waits for them, and re-layouts  36.1 us
    all_to_all x2, waiting for transfers between devices, advance(): lax.all_to_all(row_block, 'lon', split_axis=0, concat_axis=2, tiled=True)  18.2 us
    all_to_all x2, starting transfers between devices, advance(): lax.all_to_all(row_block, 'lon', split_axis=0, concat_axis=2, tiled=True)  15.1 us
    all_to_all x2, waiting for transfers between devices, advance(): lax.all_to_all(spread, 'lon', split_axis=2, concat_axis=0, tiled=True)  14.2 us
    unnamed x8, matrix products  11.3 us
    ppermute x4, starting transfers between devices, extended(): before = lax.ppermute(last, axis, up)  11.3 us
    another operation x4, local copies, waits for them, and re-layouts, truncate_rows(): folded = rows.reshape(row_count, outer, inner_factor)  10.7 us
  transfers between devices with their start and end apart: 15, of which 6 were waited for; matrix products, arithmetic and copies ran while one was open for 57% of the time, Pallas kernels for 0%

commit v1 on v0

--- a/solution.py
+++ b/solution.py
@@ -158,7 +158,10 @@
     row_limits = jnp.broadcast_to(cutoff_row, (field_count, level_count, lat_cells)).reshape(
         lon_count, -1, 1
     )
-    values = lax.all_to_all(row_block, "lon", split_axis=0, concat_axis=2, tiled=True)
+    values = jnp.concatenate(
+        lax.all_to_all(jnp.stack(jnp.split(row_block, lax.axis_size("lon"), axis=0)), "lon", 0, 0),
+        axis=2,
+    )
     limits = lax.all_to_all(row_limits, "lon", split_axis=0, concat_axis=2, tiled=True)
     spread = truncate_rows(values[0], limits[0, :, 0], lon_total)[None]
     returned = lax.all_to_all(spread, "lon", split_axis=2, concat_axis=0, tiled=True)

time: 314 us -> 338 us (1.076)
  local copies, waits for them, and re-layouts: 89.5 us -> 111 us
    unnamed x22 -> x52, local copies, waits for them, and re-layouts: 36.1 us -> 55.6 us
  transfers between devices with their start and end apart: 15 -> 15, of which waited for: 6 -> 5; matrix products, arithmetic and copies ran while one was open for 57% -> 56% of each run, Pallas kernels for 0% -> 0%
where the time goes in v1:
time: 338 us; the launch traced here: 332 us
  local copies, waits for them, and re-layouts  111 us (33%)
  other arithmetic  95.2 us (28%)
  starting transfers between devices  53.8 us (16%)
  matrix products  37.6 us (11%)
  waiting for transfers between devices  33.4 us (10%)
    unnamed x52, local copies, waits for them, and re-layouts  55.6 us
    unnamed x2, other arithmetic  55.4 us
    all_to_all x2, waiting for transfers between devices, advance(): lax.all_to_all(jnp.stack(jnp.split(row_block, lax.axis_size('lon'), axis=...  18.2 us
    all_to_all x2, starting transfers between devices, advance(): lax.all_to_all(jnp.stack(jnp.split(row_block, lax.axis_size('lon'), axis=...  15.8 us
    all_to_all x2, waiting for transfers between devices, advance(): lax.all_to_all(spread, 'lon', split_axis=2, concat_axis=0, tiled=True)  14.2 us
    unnamed x8, matrix products  11.4 us
    ppermute x4, starting transfers between devices, extended(): before = lax.ppermute(last, axis, up)  11.3 us
    another operation x4, local copies, waits for them, and re-layouts, truncate_rows(): folded = rows.reshape(row_count, outer, inner_factor)  10.7 us
  transfers between devices with their start and end apart: 15, of which 5 were waited for; matrix products, arithmetic and copies ran while one was open for 56% of the time, Pallas kernels for 0%

profile of v1, /device:TPU:9, one launch (start us, length us, event | category | flops | bytes accessed | tf_op | source)
XLA Modules:
  0.0 331.5 jit_solution(1688831620994593087)
XLA Ops:
  4.8 8.6 %all-to-all-start = ((f32[16,40,1]{1,2,0:T(1,128)}), f32[16,40,1]{1,2,0:T(1,128)S(1)}, u32[]{:S(2)}, u32[]{:S(2)}) async-start(f32[16,40,1]{1,2,0:T(1,128)} %bitcast.2), calls=%async_computation | async-start | bytes 16384 | tf_op jit(solution)/shard_map/all_to_all | solution.py:165
  17.6 1.5 copy.203
  29.2 6.0 %all-to-all-start.1 = ((f32[16,1,40,360]{3,2,1,0:T(8,128)}), f32[16,1,40,360]{3,2,1,0:T(8,128)S(1)}, u32[]{:S(2)}, u32[]{:S(2)}) async-start(f32[16,1,40,360]{3,2,1,0:T(8,128)} %constant_dynamic-update-slice_fusion.2), calls=%async_computation.1 | async-start | bytes 1966080 | tf_op jit(solution)/shard_map/all_to_all | solution.py:162
  36.4 1.5 copy.215
  37.9 2.1 collective-permute-start.2
  40.1 1.5 fusion.274
  41.6 1.5 copy.269
  44.4 1.5 copy.270
  45.9 4.0 %collective-permute-start.4 = (f32[5,1,360,3]{2,1,3,0:T(1,128)S(1)}, f32[5,1,360,3]{2,1,3,0:T(1,128)S(1)}, u32[]{:S(2)}, u32[]{:S(2)}) collective-permute-start(f32[5,1,360,3]{2,1,3,0:T(1,128)S(1)} %copy.270), channel_id=1, source_target_pairs={{0,1},{2,3},{4,5},{6,7},{8,9},{10,11},{12,13},{14,15},{16,17},{18,... | collective-permute-start | bytes 64808 | tf_op jit(solution)/shard_map/ppermute | solution.py:28
  50.2 9.0 %all-to-all-done.1 = f32[16,1,40,360]{3,2,1,0:T(8,128)S(1)} async-done(((f32[16,1,40,360]{3,2,1,0:T(8,128)}), f32[16,1,40,360]{3,2,1,0:T(8,128)S(1)}, u32[]{:S(2)}, u32[]{:S(2)}) %all-to-all-start.1) | async-done | bytes 921632 | tf_op jit(solution)/shard_map/all_to_all | solution.py:162
  60.3 3.4 %reshape_squeeze_reshape.6 = f32[40,90,64]{2,1,0:T(8,128)} reshape(f32[1,40,16,360]{3,2,1,0:T(8,128)} %copy.204) | data formatting | bytes 1843200 | tf_op jit(solution)/shard_map/reshape;squeeze;reshape | solution.py:98
  63.7 2.1 copy.205
  68.6 1.6 fusion.18
  70.2 1.6 fusion.22
  71.9 1.8 compare_select_fusion.3
  76.5 1.8 compare_select_fusion.2
  78.2 1.8 convolution_subtract_fusion.2
  80.1 1.8 multiply_add_fusion.2
  81.9 1.4 fusion.82
  83.3 1.4 fusion.90
  85.0 3.6 %copy.259 = f32[40,90,64]{0,2,1:T(8,128)} copy(f32[40,90,64]{1,2,0:T(8,128)S(1)} %multiply_bitcast_fusion.1) | data formatting | bytes 1843200 | tf_op jit(solution)/shard_map/div | solution.py:125
  89.1 27.7 %reduce = f32[5760,40]{1,0:T(8,128)} reduce(f32[5760,1,40]{2,1,0:T(1,128)} %bitcast.370, f32[]{:T(128)} %broadcast.641), dimensions={1}, to_apply=%bitcast.326.reduce_sub_computation | reduce | bytes 1843204
  116.8 4.8 %reshape.644 = f32[16,1,14400]{2,1,0:T(1,128)} reshape(f32[5760,40]{1,0:T(8,128)} %reduce) | data formatting | bytes 1843200
  121.6 5.3 %all-to-all-start.2 = ((f32[16,1,14400]{2,1,0:T(1,128)}), f32[16,1,14400]{2,1,0:T(1,128)}, u32[]{:S(2)}, u32[]{:S(2)}) async-start(f32[16,1,14400]{2,1,0:T(1,128)} %reshape.644), calls=%async_computation.2 | async-start | bytes 1851392 | tf_op jit(solution)/shard_map/all_to_all | solution.py:167
  132.9 2.8 maximum_select_fusion.1
  137.0 3.6 %subtract_multiply_fusion.1 = f32[5,1,360,129]{3,2,1,0:T(8,128)S(1)} fusion(f32[5,1,360,3]{3,2,1,0:T(8,128)S(1)} %get-tuple-element.20, f32[5,1,360,128]{3,2,1,0:T(8,128)S(1)} %copy-done, f32[5,1,360,3]{3,2,1,0:T(8,128)S(1)} %get-tuple-element.19, f32[129]{0:T(256)S(1)} %fusion.173, f32[360,129]{1,0:T(8,128)S(1)} %multiply_bitcast_fusion.4, ...), kind=kLoop, calls=%fused_computation.41 | loop fusion | flops 5572800 | bytes 2265636 | tf_op jit(solution)/shard_map/mul | solution.py:173
  140.6 8.7 %all-to-all-done.2 = f32[16,1,14400]{2,1,0:T(1,128)} async-done(((f32[16,1,14400]{2,1,0:T(1,128)}), f32[16,1,14400]{2,1,0:T(1,128)}, u32[]{:S(2)}, u32[]{:S(2)}) %all-to-all-start.2) | async-done | bytes 921632 | tf_op jit(solution)/shard_map/all_to_all | solution.py:167
  149.3 4.9 %reduce.1 = f32[16,14400]{1,0:T(8,128)} reduce(f32[16,1,14400]{2,1,0:T(1,128)} %all-to-all-done.2, f32[]{:T(128)} %broadcast.641), dimensions={1}, to_apply=%all_to_all.51.reduce_sub_computation | reduce | bytes 1843204 | tf_op jit(solution)/shard_map/all_to_all | solution.py:167
  154.3 8.8 %reshape.645 = f32[5760,1,40]{2,1,0:T(1,128)} reshape(f32[16,14400]{1,0:T(8,128)} %reduce.1) | data formatting | bytes 1843200
  163.0 3.1 copy.213
  166.1 2.5 copy.214
  168.6 1.7 fusion.36
  171.6 2.1 collective-permute-start.6
  176.9 1.5 copy.225
  188.5 9.8 %all-to-all-start.3 = ((f32[16,1,40,360]{3,2,1,0:T(8,128)}), f32[16,1,40,360]{3,2,1,0:T(8,128)S(1)}, u32[]{:S(2)}, u32[]{:S(2)}) async-start(f32[16,1,40,360]{3,2,1,0:T(8,128)} %constant_dynamic-update-slice_fusion.18), calls=%async_computation.3 | async-start | bytes 1966080 | tf_op jit(solution)/shard_map/all_to_all | solution.py:162
  198.3 1.5 fusion.270
  199.8 1.5 copy.241
  202.6 1.5 copy.244
  204.1 4.0 %collective-permute-start.9 = (f32[5,1,360,3]{2,1,3,0:T(1,128)S(1)}, f32[5,1,360,3]{2,1,3,0:T(1,128)S(1)}, u32[]{:S(2)}, u32[]{:S(2)}) collective-permute-start(f32[5,1,360,3]{2,1,3,0:T(1,128)S(1)} %copy.244), channel_id=1, source_target_pairs={{0,1},{2,3},{4,5},{6,7},{8,9},{10,11},{12,13},{14,15},{16,17},{18,... | collective-permute-start | bytes 64808 | tf_op jit(solution)/shard_map/ppermute | solution.py:28
  209.3 1.5 copy.237
  210.8 2.2 collective-permute-start.7
  213.0 9.3 %all-to-all-done.3 = f32[16,1,40,360]{3,2,1,0:T(8,128)S(1)} async-done(((f32[16,1,40,360]{3,2,1,0:T(8,128)}), f32[16,1,40,360]{3,2,1,0:T(8,128)S(1)}, u32[]{:S(2)}, u32[]{:S(2)}) %all-to-all-start.3) | async-done | bytes 921632 | tf_op jit(solution)/shard_map/all_to_all | solution.py:162
  223.4 3.4 %reshape_squeeze_reshape.7 = f32[40,90,64]{2,1,0:T(8,128)} reshape(f32[1,40,16,360]{3,2,1,0:T(8,128)} %copy.226) | data formatting | bytes 1843200 | tf_op jit(solution)/shard_map/reshape;squeeze;reshape | solution.py:98
  226.8 1.9 copy.227
  231.5 1.6 fusion.12
  233.1 1.6 fusion.16
  234.8 1.8 compare_select_fusion.1
  238.0 1.4 fusion.103
  239.4 1.8 compare_select_fusion
  241.2 1.6 convolution_subtract_fusion
  242.8 1.8 multiply_add_fusion
  244.6 1.4 fusion.86
  246.0 1.4 fusion.78
  247.7 3.6 %copy.264 = f32[40,90,64]{0,2,1:T(8,128)} copy(f32[40,90,64]{1,2,0:T(8,128)S(1)} %multiply_bitcast_fusion) | data formatting | bytes 1843200 | tf_op jit(solution)/shard_map/div | solution.py:125
  251.3 27.7 %reduce.2 = f32[5760,40]{1,0:T(8,128)} reduce(f32[5760,1,40]{2,1,0:T(1,128)} %bitcast.372, f32[]{:T(128)} %broadcast.641), dimensions={1}, to_apply=%bitcast.328.reduce_sub_computation | reduce | bytes 1843204
  279.0 4.8 %reshape.646 = f32[16,1,14400]{2,1,0:T(1,128)} reshape(f32[5760,40]{1,0:T(8,128)} %reduce.2) | data formatting | bytes 1843200
  283.8 5.1 %all-to-all-start.4 = ((f32[16,1,14400]{2,1,0:T(1,128)}), f32[16,1,14400]{2,1,0:T(1,128)S(1)}, u32[]{:S(2)}, u32[]{:S(2)}) async-start(f32[16,1,14400]{2,1,0:T(1,128)} %reshape.646), calls=%async_computation.4 | async-start | bytes 1851392 | tf_op jit(solution)/shard_map/all_to_all | solution.py:167
  296.7 3.9 %maximum_select_fusion.3 = (f32[5,1,360,3]{3,2,1,0:T(8,128)S(1)}, f32[5,1,360,3]{3,2,1,0:T(8,128)S(1)}) fusion(f32[5,1,360,3]{3,2,1,0:T(8,128)} %copy.246, f32[5,1,360,1]{3,2,1,0:T(8,128)} %copy.272, f32[5,1,360,1]{3,2,1,0:T(8,128)} %copy.271, f32[5,1,360,1]{3,2,1,0:T(8,128)} %copy.245, pred[]{:T(512)S(6)} %eq.15, f32[5,1,360,3]{3,2,1,0:T(8,128)} %copy.243, ...), kind=kLoop, calls=%fused_computation.108 | loop fusion | flops 32400 | bytes 115202 | tf_op jit(solution)/shard_map/jit(_where)/select_n | solution.py:135
  301.2 4.5 %subtract_multiply_fusion = f32[5,1,360,129]{3,2,1,0:T(8,128)} fusion(f32[5,1,360,3]{3,2,1,0:T(8,128)S(1)} %get-tuple-element.18, f32[5,1,360,128]{3,2,1,0:T(8,128)S(1)} %fusion.37, f32[5,1,360,3]{3,2,1,0:T(8,128)S(1)} %get-tuple-element.17, f32[360,129]{1,0:T(8,128)S(1)} %multiply_bitcast_fusion.2, f32[360,129]{1,0:T(8,128)S(1)} %get-tuple-element.7, ...), kind=kLoop, calls=%fused_computation.40 | loop fusion | flops 5572800 | bytes 2265636 | tf_op jit(solution)/shard_map/mul | solution.py:173
  305.7 5.5 %all-to-all-done.4 = f32[16,1,14400]{2,1,0:T(1,128)S(1)} async-done(((f32[16,1,14400]{2,1,0:T(1,128)}), f32[16,1,14400]{2,1,0:T(1,128)S(1)}, u32[]{:S(2)}, u32[]{:S(2)}) %all-to-all-start.4) | async-done | bytes 921632 | tf_op jit(solution)/shard_map/all_to_all | solution.py:167
  311.2 4.1 %reduce.3 = f32[16,14400]{1,0:T(8,128)} reduce(f32[16,1,14400]{2,1,0:T(1,128)S(1)} %all-to-all-done.4, f32[]{:T(128)} %broadcast.641), dimensions={1}, to_apply=%all_to_all.55.reduce_sub_computation | reduce | bytes 1843204 | tf_op jit(solution)/shard_map/all_to_all | solution.py:167
  315.3 8.8 %reshape.647 = f32[5760,1,40]{2,1,0:T(1,128)} reshape(f32[16,14400]{1,0:T(8,128)} %reduce.3) | data formatting | bytes 1843200
  324.1 2.3 copy.235
  327.6 2.4 fusion.34
  (138 shorter events, 70.3 us)
Async XLA Ops:
  0.0 14.7 %copy-start = (f32[5,1,360,128]{3,2,1,0:T(8,128)S(1)}, f32[5,1,360,128]{3,2,1,0:T(8,128)}, u32[]{:S(2)}) copy-start(f32[5,1,360,128]{3,2,1,0:T(8,128)} %param.4) | copy-start | bytes 2764804
  0.8 13.9 %collective-permute-start = (f32[5,1,3,128]{3,2,1,0:T(4,128)S(1)}, f32[5,1,3,128]{3,2,1,0:T(4,128)S(1)}, u32[]{:S(2)}, u32[]{:S(2)}) collective-permute-start(f32[5,1,3,128]{3,2,1,0:T(4,128)S(1)} %get-tuple-element.33), channel_id=1, source_target_pairs={{2,0},{4,2},{6,4},{8,6},{10,8},{12,10},{14,12},{16,14},{18,16},{20... | collective-permute-start | bytes 23048 | tf_op jit(solution)/shard_map/ppermute | solution.py:29
  1.5 13.2 %collective-permute-start.1 = (f32[5,1,3,128]{3,2,1,0:T(4,128)S(1)}, f32[5,1,3,128]{3,2,1,0:T(4,128)S(1)}, u32[]{:S(2)}, u32[]{:S(2)}) collective-permute-start(f32[5,1,3,128]{3,2,1,0:T(4,128)S(1)} %get-tuple-element.34), channel_id=1, source_target_pairs={{0,2},{2,4},{4,6},{6,8},{8,10},{10,12},{12,14},{14,16},{16,18},{18... | collective-permute-start | bytes 23048 | tf_op jit(solution)/shard_map/ppermute | solution.py:28
  4.8 24.4 %all-to-all-start = ((f32[16,40,1]{1,2,0:T(1,128)}), f32[16,40,1]{1,2,0:T(1,128)S(1)}, u32[]{:S(2)}, u32[]{:S(2)}) async-start(f32[16,40,1]{1,2,0:T(1,128)} %bitcast.2), calls=%async_computation | async-start | bytes 16384 | tf_op jit(solution)/shard_map/all_to_all | solution.py:165
  15.9 0.7 copy-start.1
  15.9 3.2 copy-start.2
  29.2 30.0 %all-to-all-start.1 = ((f32[16,1,40,360]{3,2,1,0:T(8,128)}), f32[16,1,40,360]{3,2,1,0:T(8,128)S(1)}, u32[]{:S(2)}, u32[]{:S(2)}) async-start(f32[16,1,40,360]{3,2,1,0:T(8,128)} %constant_dynamic-update-slice_fusion.2), calls=%async_computation.1 | async-start | bytes 1966080 | tf_op jit(solution)/shard_map/all_to_all | solution.py:162
  37.9 89.0 %collective-permute-start.2 = (f32[5,1,360,2]{2,3,1,0:T(2,128)S(1)}, f32[5,1,360,2]{2,3,1,0:T(2,128)S(1)}, u32[]{:S(2)}, u32[]{:S(2)}) collective-permute-start(f32[5,1,360,2]{2,3,1,0:T(2,128)S(1)} %copy.215), channel_id=1, source_target_pairs={{0,16},{2,18},{4,20},{6,22},{8,24},{10,26},{12,28},{14,30},{16,0},... | collective-permute-start | bytes 43208 | tf_op jit(solution)/shard_map/ppermute | solution.py:18
  43.1 84.7 %collective-permute-start.3 = (f32[5,1,360,3]{2,1,3,0:T(1,128)S(1)}, f32[5,1,360,3]{2,1,3,0:T(1,128)S(1)}, u32[]{:S(2)}, u32[]{:S(2)}) collective-permute-start(f32[5,1,360,3]{2,1,3,0:T(1,128)S(1)} %copy.269), channel_id=1, source_target_pairs={{1,0},{3,2},{5,4},{7,6},{9,8},{11,10},{13,12},{15,14},{17,16},{19,... | collective-permute-start | bytes 64808 | tf_op jit(solution)/shard_map/ppermute | solution.py:29
  45.9 83.2 %collective-permute-start.4 = (f32[5,1,360,3]{2,1,3,0:T(1,128)S(1)}, f32[5,1,360,3]{2,1,3,0:T(1,128)S(1)}, u32[]{:S(2)}, u32[]{:S(2)}) collective-permute-start(f32[5,1,360,3]{2,1,3,0:T(1,128)S(1)} %copy.270), channel_id=1, source_target_pairs={{0,1},{2,3},{4,5},{6,7},{8,9},{10,11},{12,13},{14,15},{16,17},{18,... | collective-permute-start | bytes 64808 | tf_op jit(solution)/shard_map/ppermute | solution.py:28
  121.6 5.3 %copy-start.4 = (f32[5]{0:T(128)S(1)}, f32[5]{0:T(128)}, u32[]{:S(2)}) copy-start(f32[5]{0:T(128)} %constant.123.clone) | copy-start | bytes 64
  121.6 27.7 %all-to-all-start.2 = ((f32[16,1,14400]{2,1,0:T(1,128)}), f32[16,1,14400]{2,1,0:T(1,128)}, u32[]{:S(2)}, u32[]{:S(2)}) async-start(f32[16,1,14400]{2,1,0:T(1,128)} %reshape.644), calls=%async_computation.2 | async-start | bytes 1851392 | tf_op jit(solution)/shard_map/all_to_all | solution.py:167
  170.2 1.0 copy-start.3
  171.6 3.2 collective-permute-start.5
  171.6 3.1 collective-permute-start.6
  188.5 33.8 %all-to-all-start.3 = ((f32[16,1,40,360]{3,2,1,0:T(8,128)}), f32[16,1,40,360]{3,2,1,0:T(8,128)S(1)}, u32[]{:S(2)}, u32[]{:S(2)}) async-start(f32[16,1,40,360]{3,2,1,0:T(8,128)} %constant_dynamic-update-slice_fusion.18), calls=%async_computation.3 | async-start | bytes 1966080 | tf_op jit(solution)/shard_map/all_to_all | solution.py:162
  201.3 90.2 %collective-permute-start.8 = (f32[5,1,360,3]{2,1,3,0:T(1,128)S(1)}, f32[5,1,360,3]{2,1,3,0:T(1,128)S(1)}, u32[]{:S(2)}, u32[]{:S(2)}) collective-permute-start(f32[5,1,360,3]{2,1,3,0:T(1,128)S(1)} %copy.241), channel_id=1, source_target_pairs={{1,0},{3,2},{5,4},{7,6},{9,8},{11,10},{13,12},{15,14},{17,16},{19,... | collective-permute-start | bytes 64808 | tf_op jit(solution)/shard_map/ppermute | solution.py:29
  204.1 88.7 %collective-permute-start.9 = (f32[5,1,360,3]{2,1,3,0:T(1,128)S(1)}, f32[5,1,360,3]{2,1,3,0:T(1,128)S(1)}, u32[]{:S(2)}, u32[]{:S(2)}) collective-permute-start(f32[5,1,360,3]{2,1,3,0:T(1,128)S(1)} %copy.244), channel_id=1, source_target_pairs={{0,1},{2,3},{4,5},{6,7},{8,9},{10,11},{12,13},{14,15},{16,17},{18,... | collective-permute-start | bytes 64808 | tf_op jit(solution)/shard_map/ppermute | solution.py:28
  210.8 78.0 %collective-permute-start.7 = (f32[5,1,360,2]{2,3,1,0:T(2,128)S(1)}, f32[5,1,360,2]{2,3,1,0:T(2,128)S(1)}, u32[]{:S(2)}, u32[]{:S(2)}) collective-permute-start(f32[5,1,360,2]{2,3,1,0:T(2,128)S(1)} %copy.237), channel_id=1, source_target_pairs={{0,16},{2,18},{4,20},{6,22},{8,24},{10,26},{12,28},{14,30},{16,0},... | collective-permute-start | bytes 43208 | tf_op jit(solution)/shard_map/ppermute | solution.py:18
  283.8 27.5 %all-to-all-start.4 = ((f32[16,1,14400]{2,1,0:T(1,128)}), f32[16,1,14400]{2,1,0:T(1,128)S(1)}, u32[]{:S(2)}, u32[]{:S(2)}) async-start(f32[16,1,14400]{2,1,0:T(1,128)} %reshape.646), calls=%async_computation.4 | async-start | bytes 1851392 | tf_op jit(solution)/shard_map/all_to_all | solution.py:167
